TPU v7x, 512 devices: a whole 4x4x16 slice. The times are simulated.
512 devices in a mesh: tile: 32 (over z_lo, y, core), date: 16 (over z_hi, x).
Axes of the slice: x: 4, y: 4, z: 16 (z_hi: 4, z_lo: 4; z = z_hi * 4 + z_lo), core: 2. Of those that a mesh axis runs over, the one named last changes fastest.
Arguments:
- secondary: bfloat16 [16, 2, 3072, 1024], P('date', None, 'tile'), may hold values from -6 to 6
- primary: bfloat16 [2, 3072, 1024], P(None, 'tile', 'date'), may hold values from -6 to 6
- margin_mask: int32 [3072], P('tile'), may hold values from 0 to 1, as said below
- az_off: int32 [16, 32], P('date', 'tile'), may hold values from -16 to 16
- rg_off: int32 [16, 32], P('date', 'tile'), may hold values from -16 to 16
- az_frac: float32 [16, 32], P('date', 'tile'), may hold values from 0 to 1
- rg_frac: float32 [16, 32], P('date', 'tile'), may hold values from 0 to 1
Outputs:
- looks: float32 [16, 2, 1536, 128], P('date', None, 'tile')
Inputs may be any that keep to these rules, and one draw needn't show every extreme that they name: `margin_mask`: ones lie only in the last 64 rows of each tile of 96 rows, and the last row of every tile is 1.
All inputs are finite; a program needn't handle non-finite values.
Results may differ from a plain program's by a relative error of at most 0.017.
Values may be sent and summed in bfloat16 or wider, within the bound.
A program may use at most 64 MiB of HBM per device.

v0:
```python
import jax
import jax.numpy as jnp
from jax import lax
from jax.sharding import PartitionSpec as P

KA = 16
LAG = 64
LA = 2
LR = 8


def padded(block, sides, width):
    for axis, dim in sides:
        count = lax.axis_size(axis)
        forward = [(i, i + 1) for i in range(count - 1)]
        backward = [(target, source) for source, target in forward]
        low = lax.ppermute(
            lax.slice_in_dim(block, block.shape[dim] - width, None, axis=dim), axis, forward
        )
        high = lax.ppermute(lax.slice_in_dim(block, 0, width, axis=dim), axis, backward)
        block = jnp.concatenate([low, block, high], axis=dim)
    return block


def passed_along(value, axis, steps):
    count = lax.axis_size(axis)
    initial, last = (max(0, -steps), min(count, count - steps))
    return lax.ppermute(value, axis, [(source, source + steps) for source in range(initial, last)])


def window(dist):
    return jnp.sinc(dist) * (0.5 + 0.5 * jnp.cos(jnp.pi * dist / 4.0))


def band_taps(offset, frac):
    inside = (offset >= -3) & (offset <= 4)
    return jnp.where(inside, window(offset.astype(jnp.float32) - frac), 0.0).astype(jnp.bfloat16)


def multilook(values):
    depth, rows_n, cols_n = values.shape
    return values.reshape(depth, rows_n // LA, LA, cols_n // LR, LR).mean(axis=(2, 4))


def shards(secondary, primary, margin_mask, az_off, rg_off, az_frac, rg_frac):
    rim_rows = KA + 4
    block_cols = 256
    image = secondary[0]
    rows_n = image.shape[1]
    cols_n = image.shape[2]
    extended = padded(image, (("tile", 1),), rim_rows)
    row_out = lax.broadcasted_iota(jnp.int32, (rows_n, rows_n + 2 * rim_rows), 0)
    row_in = lax.broadcasted_iota(jnp.int32, (rows_n, rows_n + 2 * rim_rows), 1)
    azim_taps = band_taps(row_in - row_out - az_off[0, 0] - rim_rows, az_frac[0, 0])
    azim = jnp.einsum(
        "im,kmc->kic", azim_taps, extended, preferred_element_type=jnp.float32
    ).astype(jnp.bfloat16)
    blocks_n = cols_n // block_cols
    col_pad = jnp.pad(azim, ((0, 0), (0, 0), (block_cols // 2, block_cols // 2)))
    pieces = col_pad.reshape(2, rows_n, blocks_n + 1, block_cols)
    inputs = jnp.concatenate([pieces[:, :, :-1], pieces[:, :, 1:]], axis=3)
    col_in = lax.broadcasted_iota(jnp.int32, (2 * block_cols, block_cols), 0)
    col_out = lax.broadcasted_iota(jnp.int32, (2 * block_cols, block_cols), 1)
    range_taps = band_taps(col_in - block_cols // 2 - col_out - rg_off[0, 0], rg_frac[0, 0])
    resampled = jnp.einsum("kibm,mn->kibn", inputs, range_taps, preferred_element_type=jnp.float32)
    resampled = resampled.reshape(2, rows_n, cols_n).astype(jnp.bfloat16)
    prim = lax.all_gather(primary, "date", axis=2, tiled=True)[None]
    moved = resampled[None]
    sec_f = moved.astype(jnp.float32)
    prim_f = prim.astype(jnp.float32)
    ifg_re = prim_f[:, 0] * sec_f[:, 0] + prim_f[:, 1] * sec_f[:, 1]
    ifg_im = prim_f[:, 1] * sec_f[:, 0] - prim_f[:, 0] * sec_f[:, 1]
    interf = jnp.stack((ifg_re, ifg_im), axis=1)
    upcoming = passed_along(interf[:, :, :LAG, :], "tile", -1)
    later = jnp.concatenate([interf[:, :, LAG:, :], upcoming], axis=2)
    l_re = later[:, 0]
    l_im = later[:, 1]
    weight = margin_mask.astype(jnp.float32)[None, :, None]
    e_re = jnp.sum(weight * (ifg_re * l_re + ifg_im * l_im), axis=(1, 2))
    e_im = jnp.sum(weight * (ifg_im * l_re - ifg_re * l_im), axis=(1, 2))
    power = jnp.sum(
        weight * 0.5 * (ifg_re * ifg_re + ifg_im * ifg_im + l_re * l_re + l_im * l_im), axis=(1, 2)
    )
    count = jnp.zeros_like(e_re) + jnp.sum(margin_mask.astype(jnp.float32)) * interf.shape[3]
    stats = jnp.stack((e_re, e_im, power, count), axis=1)
    totals = lax.psum(stats, "tile")
    magnitude = jnp.sqrt(totals[:, 0] * totals[:, 0] + totals[:, 1] * totals[:, 1])
    floor_val = (totals[:, 2] + 1e-06) / jnp.sqrt(jnp.maximum(totals[:, 3], 1.0))
    denom = jnp.maximum(magnitude, floor_val)
    u_re = (totals[:, 0] / denom)[:, None, None]
    u_im = (totals[:, 1] / denom)[:, None, None]
    c_re = multilook(ifg_re * u_re + ifg_im * u_im)
    c_im = multilook(ifg_im * u_re - ifg_re * u_im)
    result = jnp.stack((c_re, c_im), axis=1)
    return result


def solution(mesh):
    return jax.shard_map(
        shards,
        mesh=mesh,
        in_specs=(
            P("date", None, "tile", None),
            P(None, "tile", "date"),
            P("tile"),
            P("date", "tile"),
            P("date", "tile"),
            P("date", "tile"),
            P("date", "tile"),
        ),
        out_specs=P("date", None, "tile", None),
        check_vma=False,
    )
```

profile of v0, /device:TPU:1, one launch (start us, length us, event | category | flops | bytes accessed | tf_op | source)
XLA Modules:
  0.0 181.6 jit_solution(2312911935924852726)
XLA Ops:
  0.0 0.0 copy-start
  0.0 1.0 fusion.116
  1.0 4.6 %collective-permute-start = (bf16[2,20,1024]{2,1,0:T(8,128)(2,1)S(1)}, bf16[2,20,1024]{2,1,0:T(8,128)(2,1)S(1)}, u32[]{:S(2)}, u32[]{:S(2)}) collective-permute-start(bf16[2,20,1024]{2,1,0:T(8,128)(2,1)S(1)} %get-tuple-element.14), channel_id=1, source_target_pairs={{0,16},{16,32},{32,48},{48,64},{64,80},{80,96},{96,112},{112,128},... | collective-permute-start | bytes 245768 | tf_op jit(solution)/shard_map/ppermute | solution.py:17
  5.6 5.5 %collective-permute-start.1 = (bf16[2,20,1024]{2,1,0:T(8,128)(2,1)S(1)}, bf16[2,20,1024]{2,1,0:T(8,128)(2,1)S(1)}, u32[]{:S(2)}, u32[]{:S(2)}) collective-permute-start(bf16[2,20,1024]{2,1,0:T(8,128)(2,1)S(1)} %get-tuple-element.15), channel_id=1, source_target_pairs={{16,0},{32,16},{48,32},{64,48},{80,64},{96,80},{112,96},{128,112},... | collective-permute-start | bytes 245768 | tf_op jit(solution)/shard_map/ppermute | solution.py:20
  13.7 0.8 copy.15
  14.5 55.4 %all_gather.3 = bf16[2,96,1024]{1,0,2:T(2,128)(2,1)S(1)} all-gather(bf16[2,96,64]{1,0,2:T(2,128)(2,1)S(1)} %copy.15), channel_id=1, replica_groups=mesh['tile'=32,'date'=16] {'date'}, dimensions={2}, use_global_device_ids=true | all-gather | bytes 417792 | tf_op jit(solution)/shard_map/all_gather | solution.py:67
  69.9 0.4 copy.16
  70.3 0.1 bitcast_convert_fusion
  70.4 0.0 collective-permute-done
  70.4 0.0 collective-permute-done.1
  70.4 0.0 copy-done
  70.4 0.6 fusion.1
  71.1 0.3 copy.24
  71.3 0.1 pad.4.clone
  71.5 0.2 fusion.115
  71.7 0.2 copy.22
  71.9 0.2 copy.23
  72.1 2.9 %fusion = f32[2,96,4,256]{3,1,2,0:T(8,128)S(1)} fusion(bf16[2,96,4,256]{3,1,2,0:T(8,128)(2,1)S(1)} %copy.23, bf16[2,96,4,256]{3,1,2,0:T(8,128)(2,1)S(1)} %copy.22, f32[]{:T(128)} %bitcast.51, s32[]{:T(128)} %bitcast.49, s32[512]{0:T(512)S(1)} %iota_add_fusion), kind=kOutput, calls=%fused_computation.2 | convolution fusion | flops 209321984 | bytes 1574920 | tf_op jit(solution)/shard_map/kibm,mn->kibn/dot_general | solution.py:65
  75.0 0.5 copy.20
  75.5 0.4 reshape.581
  75.9 0.0 copy-start.1
  75.9 0.2 multiply_subtract_fusion.1
  76.1 3.9 %collective-permute-start.2 = (f32[1,2,64,1024]{3,2,1,0:T(8,128)S(1)}, f32[1,2,64,1024]{3,2,1,0:T(8,128)S(1)}, u32[]{:S(2)}, u32[]{:S(2)}) collective-permute-start(f32[1,2,64,1024]{3,2,1,0:T(8,128)S(1)} %pad_maximum_fusion.1), channel_id=1, source_target_pairs={{16,0},{32,16},{48,32},{64,48},{80,64},{96,80},{112,96},{128,112},... | collective-permute-start | bytes 1572872 | tf_op jit(solution)/shard_map/ppermute | solution.py:28
  80.0 0.0 copy-done.1
  80.0 0.6 broadcast_multiply_fusion
  81.3 12.3 %collective-permute-done.2 = f32[1,2,64,1024]{3,2,1,0:T(8,128)S(1)} collective-permute-done((f32[1,2,64,1024]{3,2,1,0:T(8,128)S(1)}, f32[1,2,64,1024]{3,2,1,0:T(8,128)S(1)}, u32[]{:S(2)}, u32[]{:S(2)}) %collective-permute-start.2) | collective-permute-done | bytes 524320 | tf_op jit(solution)/shard_map/ppermute | solution.py:28
  93.6 0.1 fusion.2
  93.7 1.0 fusion.29
  94.7 2.0 %pad_maximum_fusion.3 = f32[1,4]{1,0:T(1,128)S(1)} fusion(f32[1,1]{1,0:T(1,128)} %bitcast.18, f32[1,1]{1,0:T(1,128)} %bitcast.17, f32[1,1]{1,0:T(1,128)} %bitcast.15, f32[1,1]{1,0:T(1,128)} %bitcast.13), kind=kLoop, calls=%fused_computation.124 | loop fusion | flops 12 | bytes 32 | tf_op jit(solution)/shard_map/stack | solution.py:85
  96.6 61.0 %psum.7 = f32[1,4]{1,0:T(1,128)S(1)} all-reduce(f32[1,4]{1,0:T(1,128)S(1)} %pad_maximum_fusion.3), channel_id=1, replica_groups=mesh['tile'=32,'date'=16] {'tile'}, use_global_device_ids=true, to_apply=%region_4.5 | all-reduce | flops 4 | bytes 32 | tf_op jit(solution)/shard_map/psum | solution.py:86
  157.7 0.6 fusion.117
  163.6 0.1 multiply_add_fusion.1
  163.7 5.0 %add.275 = f32[48,2,128,8]{3,2,1,0:T(8,128)} reshape(f32[1,1,96,1024]{3,2,1,0:T(8,128)S(1)} %get-tuple-element.10) | data formatting | bytes 786432 | tf_op jit(solution)/shard_map/add | solution.py:92
  168.6 5.0 %sub.152 = f32[48,2,128,8]{3,2,1,0:T(8,128)} reshape(f32[1,1,96,1024]{3,2,1,0:T(8,128)S(1)} %get-tuple-element.11) | data formatting | bytes 786432 | tf_op jit(solution)/shard_map/sub | solution.py:93
  173.6 3.7 %reduce_sum.58 = f32[48,128]{1,0:T(8,128)S(1)} reduce(f32[48,2,128,8]{3,2,1,0:T(8,128)} %add.275, f32[]{:T(128)} %constant.55.clone.1), dimensions={1,3}, to_apply=%region_5.6 | reduce | flops 92160 | bytes 417796 | tf_op jit(solution)/shard_map/reduce_sum | solution.py:42
  177.3 3.7 %reduce_sum.59 = f32[48,128]{1,0:T(8,128)S(1)} reduce(f32[48,2,128,8]{3,2,1,0:T(8,128)} %sub.152, f32[]{:T(128)} %constant.55.clone.1), dimensions={1,3}, to_apply=%region_6.7 | reduce | flops 92160 | bytes 417796 | tf_op jit(solution)/shard_map/reduce_sum | solution.py:42
  181.0 0.6 pad_maximum_fusion.2
  (4 shorter events, 0.1 us)
Async XLA Ops:
  0.0 70.4 %copy-start = (bf16[1,2,96,1024]{3,2,1,0:T(8,128)(2,1)S(1)}, bf16[1,2,96,1024]{3,2,1,0:T(8,128)(2,1)}, u32[]{:S(2)}) copy-start(bf16[1,2,96,1024]{3,2,1,0:T(8,128)(2,1)} %param.7) | copy-start | bytes 1179652
  1.0 69.4 %collective-permute-start = (bf16[2,20,1024]{2,1,0:T(8,128)(2,1)S(1)}, bf16[2,20,1024]{2,1,0:T(8,128)(2,1)S(1)}, u32[]{:S(2)}, u32[]{:S(2)}) collective-permute-start(bf16[2,20,1024]{2,1,0:T(8,128)(2,1)S(1)} %get-tuple-element.14), channel_id=1, source_target_pairs={{0,16},{16,32},{32,48},{48,64},{64,80},{80,96},{96,112},{112,128},... | collective-permute-start | bytes 245768 | tf_op jit(solution)/shard_map/ppermute | solution.py:17
  5.6 64.8 %collective-permute-start.1 = (bf16[2,20,1024]{2,1,0:T(8,128)(2,1)S(1)}, bf16[2,20,1024]{2,1,0:T(8,128)(2,1)S(1)}, u32[]{:S(2)}, u32[]{:S(2)}) collective-permute-start(bf16[2,20,1024]{2,1,0:T(8,128)(2,1)S(1)} %get-tuple-element.15), channel_id=1, source_target_pairs={{16,0},{32,16},{48,32},{64,48},{80,64},{96,80},{112,96},{128,112},... | collective-permute-start | bytes 245768 | tf_op jit(solution)/shard_map/ppermute | solution.py:20
  75.9 4.1 %copy-start.1 = (s32[96]{0:T(128)S(1)}, s32[96]{0:T(128)}, u32[]{:S(2)}) copy-start(s32[96]{0:T(128)} %param.9) | copy-start | bytes 1156
  76.1 17.5 %collective-permute-start.2 = (f32[1,2,64,1024]{3,2,1,0:T(8,128)S(1)}, f32[1,2,64,1024]{3,2,1,0:T(8,128)S(1)}, u32[]{:S(2)}, u32[]{:S(2)}) collective-permute-start(f32[1,2,64,1024]{3,2,1,0:T(8,128)S(1)} %pad_maximum_fusion.1), channel_id=1, source_target_pairs={{16,0},{32,16},{48,32},{64,48},{80,64},{96,80},{112,96},{128,112},... | collective-permute-start | bytes 1572872 | tf_op jit(solution)/shard_map/ppermute | solution.py:28
where the time goes:
time: 182 us
  blocking collectives  116 us (64%)
  local copies, waits for them, and re-layouts  14.7 us (8%)
  starting transfers between devices  13.9 us (8%)
  waiting for transfers between devices  12.3 us (7%)
  other arithmetic  12 us (7%)
  between operations  8.73 us (5%)
  matrix products  3.52 us (2%)
    psum x1, blocking collectives, shards(): totals = lax.psum(stats, 'tile')  61 us
    all_gather x1, blocking collectives, shards(): prim = lax.all_gather(primary, 'date', axis=2, tiled=True)[None]  55.4 us
    ppermute x1, waiting for transfers between devices, passed_along(): lax.ppermute(value, axis, [(source, source + steps) for source in range(i...  12.3 us
    reduce_sum x2, other arithmetic, multilook(): values.reshape(depth, rows_n // LA, LA, cols_n // LR, LR).mean(axis=(2, 4))  7.34 us
    ppermute x1, starting transfers between devices, padded(): lax.ppermute(lax.slice_in_dim(block, 0, width, axis=dim), axis, backward)  5.46 us
    sub x1, local copies, waits for them, and re-layouts, shards(): c_im = multilook(ifg_im * u_re - ifg_re * u_im)  4.97 us
    add x1, local copies, waits for them, and re-layouts, shards(): c_re = multilook(ifg_re * u_re + ifg_im * u_im)  4.95 us
    ppermute x1, starting transfers between devices, padded(): lax.ppermute(lax.slice_in_dim(block, block.shape[dim] - width, None, axis...  4.58 us
  transfers between devices with their start and end apart: 3, of which 1 were waited for; matrix products, arithmetic and copies ran while one was open for 1% of the time, Pallas kernels for 0%

commit v1 on v0

--- a/solution.py
+++ b/solution.py
@@ -64,7 +64,9 @@
     range_taps = band_taps(col_in - block_cols // 2 - col_out - rg_off[0, 0], rg_frac[0, 0])
     resampled = jnp.einsum("kibm,mn->kibn", inputs, range_taps, preferred_element_type=jnp.float32)
     resampled = resampled.reshape(2, rows_n, cols_n).astype(jnp.bfloat16)
-    prim = lax.all_gather(primary, "date", axis=2, tiled=True)[None]
+    prim = jnp.concatenate(
+        lax.all_to_all(jnp.stack([primary] * lax.axis_size("date")), "date", 0, 0), axis=2
+    )[None]
     moved = resampled[None]
     sec_f = moved.astype(jnp.float32)
     prim_f = prim.astype(jnp.float32)

time: 182 us -> 155 us (0.85)
  blocking collectives: 116 us -> 64.6 us
  starting transfers between devices: 13.9 us -> 36 us
    all_gather x1 -> x0, blocking collectives: 55.4 us -> none  [shards(): prim = lax.all_gather(primary, 'date', axis=2, tiled=True)[None]]
    all_to_all x0 -> x1, starting transfers between devices: none -> 18.2 us  [shards(): lax.all_to_all(jnp.stack([primary] * lax.axis_size('date')), 'date', 0, 0)]
    ppermute x1, starting transfers between devices: 3.89 us -> 11.9 us  [passed_along(): lax.ppermute(value, axis, [(source, source + steps) for source in range(i...]
    ppermute x1, waiting for transfers between devices: 12.3 us -> 6.4 us  [passed_along(): lax.ppermute(value, axis, [(source, source + steps) for source in range(i...]
    all_to_all x0 -> x1, waiting for transfers between devices: none -> 4.76 us  [shards(): lax.all_to_all(jnp.stack([primary] * lax.axis_size('date')), 'date', 0, 0)]
    ppermute x1, starting transfers between devices: 5.46 us -> 1.92 us  [padded(): lax.ppermute(lax.slice_in_dim(block, 0, width, axis=dim), axis, backward)]
    psum x1, blocking collectives: 61 us -> 64.6 us  [shards(): totals = lax.psum(stats, 'tile')]
    sub x1 -> x2, local copies, waits for them, and re-layouts: 4.97 us -> 5.18 us  [shards(): c_im = multilook(ifg_im * u_re - ifg_re * u_im)]
  transfers between devices with their start and end apart: 3 -> 4, of which waited for: 1 -> 3; matrix products, arithmetic and copies ran while one was open for 1% -> 4% of each run, Pallas kernels for 0% -> 0%
where the time goes in v1:
time: 155 us; the launch traced here: 154 us
  blocking collectives  64.6 us (42%)
  starting transfers between devices  36 us (23%)
  local copies, waits for them, and re-layouts  15.7 us (10%)
  other arithmetic  12.6 us (8%)
  waiting for transfers between devices  12.6 us (8%)
  between operations  8.75 us (6%)
  matrix products  3.52 us (2%)
    psum x1, blocking collectives, shards(): totals = lax.psum(stats, 'tile')  64.6 us
    all_to_all x1, starting transfers between devices, shards(): lax.all_to_all(jnp.stack([primary] * lax.axis_size('date')), 'date', 0, 0)  18.2 us
    ppermute x1, starting transfers between devices, passed_along(): lax.ppermute(value, axis, [(source, source + steps) for source in range(i...  11.9 us
    reduce_sum x2, other arithmetic, multilook(): values.reshape(depth, rows_n // LA, LA, cols_n // LR, LR).mean(axis=(2, 4))  7.34 us
    ppermute x1, waiting for transfers between devices, passed_along(): lax.ppermute(value, axis, [(source, source + steps) for source in range(i...  6.4 us
    sub x2, local copies, waits for them, and re-layouts, shards(): c_im = multilook(ifg_im * u_re - ifg_re * u_im)  5.18 us
    add x2, local copies, waits for them, and re-layouts, shards(): c_re = multilook(ifg_re * u_re + ifg_im * u_im)  5.12 us
    all_to_all x1, waiting for transfers between devices, shards(): lax.all_to_all(jnp.stack([primary] * lax.axis_size('date')), 'date', 0, 0)  4.76 us
  transfers between devices with their start and end apart: 4, of which 3 were waited for; matrix products, arithmetic and copies ran while one was open for 4% of the time, Pallas kernels for 0%

profile of v1, /device:TPU:1, one launch (start us, length us, event | category | flops | bytes accessed | tf_op | source)
XLA Modules:
  0.0 153.7 jit_solution(3965809137271125351)
XLA Ops:
  0.0 0.0 copy-start
  0.0 1.7 %stack.14 = bf16[16,2,96,64]{2,3,1,0:T(8,128)(2,1)} broadcast(bf16[2,96,64]{1,2,0:T(8,128)(2,1)} %param.8), dimensions={1,2,3} | broadcast | bytes 417792 | tf_op jit(solution)/shard_map/stack | solution.py:68
  1.7 18.2 %all-to-all-start = ((bf16[16,2,96,64]{2,3,1,0:T(8,128)(2,1)}), bf16[16,2,96,64]{2,3,1,0:T(8,128)(2,1)S(1)}, u32[]{:S(2)}, u32[]{:S(2)}) async-start(bf16[16,2,96,64]{2,3,1,0:T(8,128)(2,1)} %stack.14), calls=%async_computation | async-start | bytes 1048576 | tf_op jit(solution)/shard_map/all_to_all | solution.py:68
  19.9 0.0 copy-done
  20.0 4.0 %collective-permute-start = (bf16[2,20,1024]{2,1,0:T(8,128)(2,1)S(1)}, bf16[2,20,1024]{2,1,0:T(8,128)(2,1)S(1)}, u32[]{:S(2)}, u32[]{:S(2)}) collective-permute-start(bf16[2,20,1024]{2,1,0:T(8,128)(2,1)S(1)} %get-tuple-element.14), channel_id=1, source_target_pairs={{0,16},{16,32},{32,48},{48,64},{64,80},{80,96},{96,112},{112,128},... | collective-permute-start | bytes 245768 | tf_op jit(solution)/shard_map/ppermute | solution.py:17
  24.0 1.9 %collective-permute-start.1 = (bf16[2,20,1024]{2,1,0:T(8,128)(2,1)S(1)}, bf16[2,20,1024]{2,1,0:T(8,128)(2,1)S(1)}, u32[]{:S(2)}, u32[]{:S(2)}) collective-permute-start(bf16[2,20,1024]{2,1,0:T(8,128)(2,1)S(1)} %get-tuple-element.15), channel_id=1, source_target_pairs={{16,0},{32,16},{48,32},{64,48},{80,64},{96,80},{112,96},{128,112},... | collective-permute-start | bytes 245768 | tf_op jit(solution)/shard_map/ppermute | solution.py:20
  28.5 0.0 collective-permute-done
  28.6 1.4 collective-permute-done.1
  30.0 0.6 fusion.1
  30.6 0.3 copy.35
  30.9 0.1 pad.4.clone
  31.0 0.2 fusion.115
  31.2 0.2 copy.33
  31.4 0.2 copy.34
  31.6 2.9 %fusion = f32[2,96,4,256]{3,1,2,0:T(8,128)S(1)} fusion(bf16[2,96,4,256]{3,1,2,0:T(8,128)(2,1)S(1)} %copy.34, bf16[2,96,4,256]{3,1,2,0:T(8,128)(2,1)S(1)} %copy.33, f32[]{:T(128)} %bitcast.52, s32[]{:T(128)} %bitcast.50, s32[512]{0:T(512)S(1)} %iota_add_fusion), kind=kOutput, calls=%fused_computation.2 | convolution fusion | flops 209321984 | bytes 1574920 | tf_op jit(solution)/shard_map/kibm,mn->kibn/dot_general | solution.py:65
  34.5 0.3 copy.31
  34.8 4.8 %all-to-all-done = bf16[16,2,96,64]{2,3,1,0:T(8,128)(2,1)S(1)} async-done(((bf16[16,2,96,64]{2,3,1,0:T(8,128)(2,1)}), bf16[16,2,96,64]{2,3,1,0:T(8,128)(2,1)S(1)}, u32[]{:S(2)}, u32[]{:S(2)}) %all-to-all-start) | async-done | bytes 393248 | tf_op jit(solution)/shard_map/all_to_all | solution.py:68
  39.6 0.1 convert_bitcast_fusion
  39.7 0.1 copy.19
  39.8 0.1 multiply_subtract_fusion.1
  39.9 0.0 copy-start.1
  39.9 0.1 pad_maximum_fusion
  40.0 0.3 copy.26
  40.3 11.9 %collective-permute-start.2 = (f32[1,2,64,1024]{3,2,1,0:T(8,128)S(1)}, f32[1,2,64,1024]{3,2,1,0:T(8,128)}, u32[]{:S(2)}, u32[]{:S(2)}) collective-permute-start(f32[1,2,64,1024]{3,2,1,0:T(8,128)S(1)} %copy.26), channel_id=1, source_target_pairs={{16,0},{32,16},{48,32},{64,48},{80,64},{96,80},{112,96},{128,112},... | collective-permute-start | bytes 1572872 | tf_op jit(solution)/shard_map/ppermute | solution.py:28
  52.2 0.0 copy-done.1
  52.2 0.6 broadcast_multiply_fusion
  53.5 0.3 slice_maximum_fusion
  53.8 6.4 %collective-permute-done.2 = f32[1,2,64,1024]{3,2,1,0:T(8,128)} collective-permute-done((f32[1,2,64,1024]{3,2,1,0:T(8,128)S(1)}, f32[1,2,64,1024]{3,2,1,0:T(8,128)}, u32[]{:S(2)}, u32[]{:S(2)}) %collective-permute-start.2) | collective-permute-done | bytes 524320 | tf_op jit(solution)/shard_map/ppermute | solution.py:28
  60.2 1.4 copy.27
  61.6 1.3 fusion.21
  62.9 2.0 %pad_maximum_fusion.3 = f32[1,4]{1,0:T(1,128)S(1)} fusion(f32[1,1]{1,0:T(1,128)} %bitcast.18, f32[1,1]{1,0:T(1,128)} %bitcast.17, f32[1,1]{1,0:T(1,128)} %bitcast.15, f32[1,1]{1,0:T(1,128)} %bitcast.13), kind=kLoop, calls=%fused_computation.127 | loop fusion | flops 12 | bytes 32 | tf_op jit(solution)/shard_map/stack | solution.py:87
  64.8 64.6 %psum.7 = f32[1,4]{1,0:T(1,128)S(1)} all-reduce(f32[1,4]{1,0:T(1,128)S(1)} %pad_maximum_fusion.3), channel_id=1, replica_groups=mesh['tile'=32,'date'=16] {'tile'}, use_global_device_ids=true, to_apply=%region_4.5 | all-reduce | flops 4 | bytes 32 | tf_op jit(solution)/shard_map/psum | solution.py:88
  129.4 0.6 fusion.117
  135.3 0.1 multiply_add_fusion.1
  135.4 0.2 copy.28
  135.6 0.2 copy.29
  135.8 5.0 %sub.152 = f32[48,2,128,8]{3,2,1,0:T(8,128)} reshape(f32[1,1,96,1024]{3,2,1,0:T(8,128)S(1)} %copy.29) | data formatting | bytes 786432 | tf_op jit(solution)/shard_map/sub | solution.py:95
  140.8 4.9 %add.275 = f32[48,2,128,8]{3,2,1,0:T(8,128)} reshape(f32[1,1,96,1024]{3,2,1,0:T(8,128)S(1)} %copy.28) | data formatting | bytes 786432 | tf_op jit(solution)/shard_map/add | solution.py:94
  145.8 3.7 %reduce_sum.59 = f32[48,128]{1,0:T(8,128)S(1)} reduce(f32[48,2,128,8]{3,2,1,0:T(8,128)} %sub.152, f32[]{:T(128)} %constant.55.clone.1), dimensions={1,3}, to_apply=%region_6.7 | reduce | flops 92160 | bytes 417796 | tf_op jit(solution)/shard_map/reduce_sum | solution.py:42
  149.4 3.7 %reduce_sum.58 = f32[48,128]{1,0:T(8,128)S(1)} reduce(f32[48,2,128,8]{3,2,1,0:T(8,128)} %add.275, f32[]{:T(128)} %constant.55.clone.1), dimensions={1,3}, to_apply=%region_5.6 | reduce | flops 92160 | bytes 417796 | tf_op jit(solution)/shard_map/reduce_sum | solution.py:42
  153.1 0.6 pad_maximum_fusion.2
  (4 shorter events, 0.0 us)
Async XLA Ops:
  0.0 19.9 %copy-start = (bf16[1,2,96,1024]{3,2,1,0:T(8,128)(2,1)S(1)}, bf16[1,2,96,1024]{3,2,1,0:T(8,128)(2,1)}, u32[]{:S(2)}) copy-start(bf16[1,2,96,1024]{3,2,1,0:T(8,128)(2,1)} %param.7) | copy-start | bytes 1179652
  1.7 37.9 %all-to-all-start = ((bf16[16,2,96,64]{2,3,1,0:T(8,128)(2,1)}), bf16[16,2,96,64]{2,3,1,0:T(8,128)(2,1)S(1)}, u32[]{:S(2)}, u32[]{:S(2)}) async-start(bf16[16,2,96,64]{2,3,1,0:T(8,128)(2,1)} %stack.14), calls=%async_computation | async-start | bytes 1048576 | tf_op jit(solution)/shard_map/all_to_all | solution.py:68
  20.0 8.6 %collective-permute-start = (bf16[2,20,1024]{2,1,0:T(8,128)(2,1)S(1)}, bf16[2,20,1024]{2,1,0:T(8,128)(2,1)S(1)}, u32[]{:S(2)}, u32[]{:S(2)}) collective-permute-start(bf16[2,20,1024]{2,1,0:T(8,128)(2,1)S(1)} %get-tuple-element.14), channel_id=1, source_target_pairs={{0,16},{16,32},{32,48},{48,64},{64,80},{80,96},{96,112},{112,128},... | collective-permute-start | bytes 245768 | tf_op jit(solution)/shard_map/ppermute | solution.py:17
  24.0 5.9 %collective-permute-start.1 = (bf16[2,20,1024]{2,1,0:T(8,128)(2,1)S(1)}, bf16[2,20,1024]{2,1,0:T(8,128)(2,1)S(1)}, u32[]{:S(2)}, u32[]{:S(2)}) collective-permute-start(bf16[2,20,1024]{2,1,0:T(8,128)(2,1)S(1)} %get-tuple-element.15), channel_id=1, source_target_pairs={{16,0},{32,16},{48,32},{64,48},{80,64},{96,80},{112,96},{128,112},... | collective-permute-start | bytes 245768 | tf_op jit(solution)/shard_map/ppermute | solution.py:20
  39.9 12.3 %copy-start.1 = (s32[96]{0:T(128)S(1)}, s32[96]{0:T(128)}, u32[]{:S(2)}) copy-start(s32[96]{0:T(128)} %param.9) | copy-start | bytes 1156
  40.3 19.9 %collective-permute-start.2 = (f32[1,2,64,1024]{3,2,1,0:T(8,128)S(1)}, f32[1,2,64,1024]{3,2,1,0:T(8,128)}, u32[]{:S(2)}, u32[]{:S(2)}) collective-permute-start(f32[1,2,64,1024]{3,2,1,0:T(8,128)S(1)} %copy.26), channel_id=1, source_target_pairs={{16,0},{32,16},{48,32},{64,48},{80,64},{96,80},{112,96},{128,112},... | collective-permute-start | bytes 1572872 | tf_op jit(solution)/shard_map/ppermute | solution.py:28
